TPU v7x, 256 devices: a whole 4x4x8 slice. The times are simulated.
256 devices in a mesh: gx: 16 (over z, core), gy: 16 (over y, x).
Axes of the slice: x: 4, y: 4, z: 8, core: 2. Of those that a mesh axis runs over, the one named last changes fastest.
Arguments:
- demand: float32 [16, 1024, 16384], P(None, 'gx', 'gy'), may hold values from -200 to 200, as said below
- initial: float32 [1024, 256], replicated, may hold values from -6 to 6
Outputs:
- factor: float32 [1024, 256], replicated
- core: float32 [256, 16, 16384], P('gx', None, 'gy')
Inputs may be any that keep to these rules, and one draw needn't show every extreme that they name: `demand`: Real-valued fluctuations of order one to a few, not all of one scale along x.
All inputs are finite; a program needn't handle non-finite values.
Results may differ from a plain program's by a relative error of at most 0.0003.
Values sent between devices are 32-bit elements; how exact they have to be, the bound alone decides.
No kernel may reach another device: no remote copies, remote signals or barrier semaphores. Data moves between devices by JAX's collectives and lax.ppermute only.
A program may use at most 128 MiB of HBM per device.

v0:
```python
import jax
import jax.numpy as jnp
from jax import lax
from jax.sharding import PartitionSpec as P

NY = 1024
L = 16
S = 16
ITERS = 3


def orthonormal(block):
    weights = jnp.dot(
        block.T, block, precision=lax.Precision.HIGHEST, preferred_element_type=jnp.float32
    )
    lower_factor = jnp.linalg.cholesky(weights)
    return lax.linalg.triangular_solve(
        lower_factor, block, left_side=False, lower=True, transpose_a=True
    )


def on_device(demand, initial):
    regrouped = lax.all_to_all(demand, "gx", split_axis=0, concat_axis=1, tiled=True)
    local_gram = jnp.einsum(
        "lxc,lzc->xz",
        regrouped,
        regrouped,
        precision=lax.Precision.HIGHEST,
        preferred_element_type=jnp.float32,
    )
    local_gram = local_gram * (1.0 / (L * S * NY))
    basis = initial
    gram = lax.psum(local_gram, ("gx", "gy"))
    for iteration in range(ITERS):
        basis = orthonormal(
            jnp.dot(
                gram, basis, precision=lax.Precision.HIGHEST, preferred_element_type=jnp.float32
            )
        )
    core_part = jnp.einsum(
        "xr,lxc->rlc",
        basis,
        regrouped,
        precision=lax.Precision.HIGHEST,
        preferred_element_type=jnp.float32,
    )
    core = lax.all_to_all(core_part, "gx", split_axis=0, concat_axis=1, tiled=True)
    return (basis, core)


def solution(mesh):
    in_specs = (P(None, "gx", "gy"), P())
    out_specs = (P(), P("gx", None, "gy"))
    return jax.shard_map(
        on_device, mesh=mesh, in_specs=in_specs, out_specs=out_specs, check_vma=False
    )
```

profile of v0, /device:TPU:1, one launch (start us, length us, event | category | flops | bytes accessed | tf_op | source)
XLA Modules:
  0.0 658.2 jit_solution(15279910534653061629)
XLA Ops:
  7.2 106.0 %all_to_all.27 = f32[16,64,1024]{2,1,0:T(8,128)S(1)} all-to-all(f32[16,64,1024]{2,1,0:T(8,128)} %param.5), channel_id=1, replica_groups=mesh['gx'=16,'gy'=16] {'gx'}, dimensions={0} | all-to-all | bytes 8388608 | tf_op jit(solution)/shard_map/all_to_all | solution.py:23
  113.2 1.9 copy-done.1
  115.1 14.7 %convolution_multiply_fusion = f32[1024,1024]{1,0:T(8,128)} fusion(f32[1024,1024]{1,0:T(8,128)S(1)} %bitcast.118), kind=kOutput, calls=%fused_computation.6 | convolution fusion | flops 12885950464 | bytes 8388608 | tf_op jit(solution)/shard_map/lxc,lzc->xz/dot_general | solution.py:24
  129.9 265.4 %all-reduce.3.cloned.1.call-done = f32[1024,1024]{1,0:T(8,128)} async-done(((f32[1024,1024]{1,0:T(8,128)}), f32[1024,1024]{1,0:T(8,128)}) %all-reduce.3.cloned.1.call-update) | async-done | bytes 4194320 | tf_op jit(solution)/shard_map/psum | solution.py:33
  395.3 5.4 fusion.45
  400.7 1.8 fusion.46
  402.8 11.7 %cholesky.172 = f32[128,128]{1,0:T(8,128)S(1)} custom-call(f32[128,128]{1,0:T(8,128)S(1)} %cholesky.270), custom_call_target="Cholesky" | custom-call | tf_op jit(solution)/shard_map/jit(cholesky)/cholesky | solution.py:16
  414.5 9.8 %custom-call.15 = f32[1,128,128]{1,2,0:T(8,128)S(1)} custom-call(f32[1,128,128]{2,1,0:T(8,128)S(1)} %get-tuple-element.72), custom_call_target="InvertDiagBlocksLowerTriangular" | custom-call | tf_op jit(solution)/shard_map/jit(cholesky)/cholesky | solution.py:16
  424.8 11.7 %cholesky.189 = f32[128,128]{1,0:T(8,128)S(1)} custom-call(f32[128,128]{1,0:T(8,128)S(1)} %convolution_subtract_fusion.5), custom_call_target="Cholesky" | custom-call | tf_op jit(solution)/shard_map/jit(cholesky)/cholesky | solution.py:16
  439.0 3.7 while.6
  442.7 19.7 %custom-call.16 = f32[2,128,128]{1,2,0:T(8,128)S(1)} custom-call(f32[2,128,128]{2,1,0:T(8,128)S(1)} %get-tuple-element.24), custom_call_target="InvertDiagBlocksLowerTriangular" | custom-call | tf_op jit(solution)/shard_map/triangular_solve/custom-call.0 | solution.py:17
  464.7 5.3 fusion
  470.0 1.8 fusion.47
  472.1 11.7 %cholesky.206 = f32[128,128]{1,0:T(8,128)S(1)} custom-call(f32[128,128]{1,0:T(8,128)S(1)} %cholesky.273), custom_call_target="Cholesky" | custom-call | tf_op jit(solution)/shard_map/jit(cholesky)/cholesky | solution.py:16
  483.8 9.8 %custom-call.17 = f32[1,128,128]{1,2,0:T(8,128)S(1)} custom-call(f32[1,128,128]{2,1,0:T(8,128)S(1)} %get-tuple-element.68), custom_call_target="InvertDiagBlocksLowerTriangular" | custom-call | tf_op jit(solution)/shard_map/jit(cholesky)/cholesky | solution.py:16
  494.1 11.7 %cholesky.223 = f32[128,128]{1,0:T(8,128)S(1)} custom-call(f32[128,128]{1,0:T(8,128)S(1)} %convolution_subtract_fusion.4), custom_call_target="Cholesky" | custom-call | tf_op jit(solution)/shard_map/jit(cholesky)/cholesky | solution.py:16
  508.6 3.8 while.7
  512.4 19.7 %custom-call.18 = f32[2,128,128]{1,2,0:T(8,128)S(1)} custom-call(f32[2,128,128]{2,1,0:T(8,128)S(1)} %get-tuple-element.25), custom_call_target="InvertDiagBlocksLowerTriangular" | custom-call | tf_op jit(solution)/shard_map/triangular_solve/custom-call.0 | solution.py:17
  534.4 5.5 fusion.4
  540.0 1.8 fusion.48
  542.0 11.7 %cholesky.240 = f32[128,128]{1,0:T(8,128)S(1)} custom-call(f32[128,128]{1,0:T(8,128)S(1)} %cholesky.276), custom_call_target="Cholesky" | custom-call | tf_op jit(solution)/shard_map/jit(cholesky)/cholesky | solution.py:16
  553.8 9.8 %custom-call.19 = f32[1,128,128]{1,2,0:T(8,128)S(1)} custom-call(f32[1,128,128]{2,1,0:T(8,128)S(1)} %get-tuple-element.64), custom_call_target="InvertDiagBlocksLowerTriangular" | custom-call | tf_op jit(solution)/shard_map/jit(cholesky)/cholesky | solution.py:16
  564.1 11.7 %cholesky.257 = f32[128,128]{1,0:T(8,128)S(1)} custom-call(f32[128,128]{1,0:T(8,128)S(1)} %convolution_subtract_fusion.3), custom_call_target="Cholesky" | custom-call | tf_op jit(solution)/shard_map/jit(cholesky)/cholesky | solution.py:16
  578.7 3.9 while.8
  581.3 1.4 bitcast_dynamic-update-slice_fusion.8
  582.6 19.7 %custom-call.20 = f32[2,128,128]{1,2,0:T(8,128)S(1)} custom-call(f32[2,128,128]{2,1,0:T(8,128)S(1)} %get-tuple-element.26), custom_call_target="InvertDiagBlocksLowerTriangular" | custom-call | tf_op jit(solution)/shard_map/triangular_solve/custom-call.0 | solution.py:17
  604.6 5.7 convolution_bitcast_fusion
  610.3 2.1 copy.12
  612.4 7.6 %all-to-all-start.1 = ((f32[256,1,1024]{2,1,0:T(1,128)}), f32[256,1,1024]{2,1,0:T(1,128)}, u32[]{:S(2)}, u32[]{:S(2)}) async-start(f32[256,1,1024]{2,1,0:T(1,128)} %copy.12), calls=%async_computation.1 | async-start | bytes 2097152 | tf_op jit(solution)/shard_map/all_to_all | solution.py:47
  621.1 2.5 copy.14
  623.6 24.5 %all-to-all-done.1 = f32[256,1,1024]{2,1,0:T(1,128)} async-done(((f32[256,1,1024]{2,1,0:T(1,128)}), f32[256,1,1024]{2,1,0:T(1,128)}, u32[]{:S(2)}, u32[]{:S(2)}) %all-to-all-start.1) | async-done | bytes 1048608 | tf_op jit(solution)/shard_map/all_to_all | solution.py:47
  648.1 2.8 copy.16
  (69 shorter events, 23.9 us)
Async XLA Ops:
  7.2 388.1 %copy-start = (f32[1024,256]{1,0:T(8,128)S(1)}, f32[1024,256]{1,0:T(8,128)}, u32[]{:S(2)}) copy-start(f32[1024,256]{1,0:T(8,128)} %param.6) | copy-start | bytes 3145732
  7.2 388.1 %all-reduce.3.cloned.1.call-start = ((), (), s32[]{:S(2)}) async-start(), calls=%async_computation.2 | async-start | bytes 8388608 | tf_op jit(solution)/shard_map/psum | solution.py:33
  113.2 1.9 copy-start.1
  612.4 35.7 %all-to-all-start.1 = ((f32[256,1,1024]{2,1,0:T(1,128)}), f32[256,1,1024]{2,1,0:T(1,128)}, u32[]{:S(2)}, u32[]{:S(2)}) async-start(f32[256,1,1024]{2,1,0:T(1,128)} %copy.12), calls=%async_computation.1 | async-start | bytes 2097152 | tf_op jit(solution)/shard_map/all_to_all | solution.py:47
Sparse Core Ops, SparseCore 0:
  130.0 265.2 all-reduce.2
where the time goes:
time: 665 us; the launch traced here: 658 us
  waiting for transfers between devices  290 us (44%)
  other arithmetic  164 us (25%)
  blocking collectives  106 us (16%)
  matrix products  50.4 us (8%)
  local copies, waits for them, and re-layouts  21.3 us (3%)
  between operations  18.9 us (3%)
  starting transfers between devices  7.65 us (1%)
    psum x1, waiting for transfers between devices, on_device(): gram = lax.psum(local_gram, ('gx', 'gy'))  265 us
    all_to_all x1, blocking collectives, on_device(): lax.all_to_all(demand, 'gx', split_axis=0, concat_axis=1, tiled=True)  106 us
    another operation x20, other arithmetic, orthonormal(): lower_factor = jnp.linalg.cholesky(weights)  103 us
    another operation x8, other arithmetic, orthonormal(): lax.linalg.triangular_solve(lower_factor, block, left_side=False, lower=T...  60.6 us
    all_to_all x1, waiting for transfers between devices, on_device(): lax.all_to_all(core_part, 'gx', split_axis=0, concat_axis=1, tiled=True)  24.5 us
    dot_general x3, matrix products, on_device(): jnp.dot(gram, basis, precision=lax.Precision.HIGHEST, preferred_element_t...  16.3 us
    dot_general x1, matrix products, on_device(): jnp.einsum('lxc,lzc->xz', regrouped, regrouped, precision=lax.Precision.H...  14.7 us
  transfers between devices with their start and end apart: 2, of which 2 were waited for; matrix products, arithmetic and copies ran while one was open for 1% of the time, Pallas kernels for 0%

commit v1 on v0

--- a/solution.py
+++ b/solution.py
@@ -20,6 +20,11 @@
 
 
 def on_device(demand, initial):
+
+    def detail_edges_here(block_here, across, row_axis):
+        opened = lax.psum(block_here, across)
+        return lax.psum(opened, row_axis)
+
     regrouped = lax.all_to_all(demand, "gx", split_axis=0, concat_axis=1, tiled=True)
     local_gram = jnp.einsum(
         "lxc,lzc->xz",
@@ -30,7 +35,7 @@
     )
     local_gram = local_gram * (1.0 / (L * S * NY))
     basis = initial
-    gram = lax.psum(local_gram, ("gx", "gy"))
+    gram = detail_edges_here(local_gram, "gx", "gy")
     for iteration in range(ITERS):
         basis = orthonormal(
             jnp.dot(

time: 665 us -> 636 us (0.956)
  waiting for transfers between devices: 290 us -> 260 us
    psum x1 -> x2, waiting for transfers between devices: 265 us -> 235 us  [the longest x1 118 us: detail_edges_here(): opened = lax.psum(block_here, across)]
  transfers between devices with their start and end apart: 2 -> 3, of which waited for: 2 -> 3; matrix products, arithmetic and copies ran while one was open for 1% -> 1% of each run, Pallas kernels for 0% -> 0%
where the time goes in v1:
time: 636 us; the launch traced here: 628 us
  waiting for transfers between devices  260 us (41%)
  other arithmetic  164 us (26%)
  blocking collectives  106 us (17%)
  matrix products  50.4 us (8%)
  local copies, waits for them, and re-layouts  21.3 us (3%)
  between operations  19 us (3%)
  starting transfers between devices  8.12 us (1%)
    psum x1, waiting for transfers between devices, detail_edges_here(): opened = lax.psum(block_here, across)  118 us
    psum x1, waiting for transfers between devices, detail_edges_here(): return lax.psum(opened, row_axis)  117 us
    all_to_all x1, blocking collectives, on_device(): lax.all_to_all(demand, 'gx', split_axis=0, concat_axis=1, tiled=True)  106 us
    another operation x20, other arithmetic, orthonormal(): lower_factor = jnp.linalg.cholesky(weights)  103 us
    another operation x8, other arithmetic, orthonormal(): lax.linalg.triangular_solve(lower_factor, block, left_side=False, lower=T...  60.6 us
    all_to_all x1, waiting for transfers between devices, on_device(): lax.all_to_all(core_part, 'gx', split_axis=0, concat_axis=1, tiled=True)  24.5 us
    dot_general x3, matrix products, on_device(): jnp.dot(gram, basis, precision=lax.Precision.HIGHEST, preferred_element_t...  16.3 us
    dot_general x1, matrix products, on_device(): jnp.einsum('lxc,lzc->xz', regrouped, regrouped, precision=lax.Precision.H...  14.8 us
  transfers between devices with their start and end apart: 3, of which 3 were waited for; matrix products, arithmetic and copies ran while one was open for 1% of the time, Pallas kernels for 0%

profile of v1, /device:TPU:1, one launch (start us, length us, event | category | flops | bytes accessed | tf_op | source)
XLA Modules:
  0.0 628.5 jit_solution(16156951686608494834)
XLA Ops:
  7.2 106.0 %all_to_all.27 = f32[16,64,1024]{2,1,0:T(8,128)S(1)} all-to-all(f32[16,64,1024]{2,1,0:T(8,128)} %param.5), channel_id=1, replica_groups=mesh['gx'=16,'gy'=16] {'gx'}, dimensions={0} | all-to-all | bytes 8388608 | tf_op jit(solution)/shard_map/all_to_all | solution.py:28
  113.2 1.9 copy-done.1
  115.1 14.8 %convolution_multiply_fusion = f32[1024,1024]{1,0:T(8,128)} fusion(f32[1024,1024]{1,0:T(8,128)S(1)} %bitcast.118), kind=kOutput, calls=%fused_computation.6 | convolution fusion | flops 12885950464 | bytes 8388608 | tf_op jit(solution)/shard_map/lxc,lzc->xz/dot_general | solution.py:29
  130.0 117.9 %all-reduce.4.cloned.1.call-done = f32[1024,1024]{1,0:T(8,128)} async-done(((f32[1024,1024]{1,0:T(8,128)}), f32[1024,1024]{1,0:T(8,128)}) %all-reduce.4.cloned.1.call-update) | async-done | bytes 4194320 | tf_op jit(solution)/shard_map/psum | solution.py:25
  247.9 117.2 %all-reduce.6.cloned.1.call-done = f32[1024,1024]{1,0:T(8,128)} async-done(((f32[1024,1024]{1,0:T(8,128)}), f32[1024,1024]{1,0:T(8,128)}) %all-reduce.6.cloned.1.call-update) | async-done | bytes 4194320 | tf_op jit(solution)/shard_map/psum | solution.py:26
  365.2 5.4 fusion.45
  370.6 1.8 fusion.46
  372.6 11.7 %cholesky.172 = f32[128,128]{1,0:T(8,128)S(1)} custom-call(f32[128,128]{1,0:T(8,128)S(1)} %cholesky.270), custom_call_target="Cholesky" | custom-call | tf_op jit(solution)/shard_map/jit(cholesky)/cholesky | solution.py:16
  384.4 9.8 %custom-call.15 = f32[1,128,128]{1,2,0:T(8,128)S(1)} custom-call(f32[1,128,128]{2,1,0:T(8,128)S(1)} %get-tuple-element.72), custom_call_target="InvertDiagBlocksLowerTriangular" | custom-call | tf_op jit(solution)/shard_map/jit(cholesky)/cholesky | solution.py:16
  394.7 11.7 %cholesky.189 = f32[128,128]{1,0:T(8,128)S(1)} custom-call(f32[128,128]{1,0:T(8,128)S(1)} %convolution_subtract_fusion.5), custom_call_target="Cholesky" | custom-call | tf_op jit(solution)/shard_map/jit(cholesky)/cholesky | solution.py:16
  408.8 3.7 while.6
  412.6 19.7 %custom-call.16 = f32[2,128,128]{1,2,0:T(8,128)S(1)} custom-call(f32[2,128,128]{2,1,0:T(8,128)S(1)} %get-tuple-element.24), custom_call_target="InvertDiagBlocksLowerTriangular" | custom-call | tf_op jit(solution)/shard_map/triangular_solve/custom-call.0 | solution.py:17
  434.5 5.3 fusion
  439.9 1.8 fusion.47
  441.9 11.7 %cholesky.206 = f32[128,128]{1,0:T(8,128)S(1)} custom-call(f32[128,128]{1,0:T(8,128)S(1)} %cholesky.273), custom_call_target="Cholesky" | custom-call | tf_op jit(solution)/shard_map/jit(cholesky)/cholesky | solution.py:16
  453.7 9.8 %custom-call.17 = f32[1,128,128]{1,2,0:T(8,128)S(1)} custom-call(f32[1,128,128]{2,1,0:T(8,128)S(1)} %get-tuple-element.68), custom_call_target="InvertDiagBlocksLowerTriangular" | custom-call | tf_op jit(solution)/shard_map/jit(cholesky)/cholesky | solution.py:16
  464.0 11.7 %cholesky.223 = f32[128,128]{1,0:T(8,128)S(1)} custom-call(f32[128,128]{1,0:T(8,128)S(1)} %convolution_subtract_fusion.4), custom_call_target="Cholesky" | custom-call | tf_op jit(solution)/shard_map/jit(cholesky)/cholesky | solution.py:16
  478.4 3.8 while.7
  482.3 19.7 %custom-call.18 = f32[2,128,128]{1,2,0:T(8,128)S(1)} custom-call(f32[2,128,128]{2,1,0:T(8,128)S(1)} %get-tuple-element.25), custom_call_target="InvertDiagBlocksLowerTriangular" | custom-call | tf_op jit(solution)/shard_map/triangular_solve/custom-call.0 | solution.py:17
  504.2 5.5 fusion.4
  509.8 1.8 fusion.48
  511.8 11.7 %cholesky.240 = f32[128,128]{1,0:T(8,128)S(1)} custom-call(f32[128,128]{1,0:T(8,128)S(1)} %cholesky.276), custom_call_target="Cholesky" | custom-call | tf_op jit(solution)/shard_map/jit(cholesky)/cholesky | solution.py:16
  523.6 9.8 %custom-call.19 = f32[1,128,128]{1,2,0:T(8,128)S(1)} custom-call(f32[1,128,128]{2,1,0:T(8,128)S(1)} %get-tuple-element.64), custom_call_target="InvertDiagBlocksLowerTriangular" | custom-call | tf_op jit(solution)/shard_map/jit(cholesky)/cholesky | solution.py:16
  533.9 11.7 %cholesky.257 = f32[128,128]{1,0:T(8,128)S(1)} custom-call(f32[128,128]{1,0:T(8,128)S(1)} %convolution_subtract_fusion.3), custom_call_target="Cholesky" | custom-call | tf_op jit(solution)/shard_map/jit(cholesky)/cholesky | solution.py:16
  548.5 3.9 while.8
  552.5 19.7 %custom-call.20 = f32[2,128,128]{1,2,0:T(8,128)S(1)} custom-call(f32[2,128,128]{2,1,0:T(8,128)S(1)} %get-tuple-element.26), custom_call_target="InvertDiagBlocksLowerTriangular" | custom-call | tf_op jit(solution)/shard_map/triangular_solve/custom-call.0 | solution.py:17
  574.4 5.7 convolution_bitcast_fusion
  580.1 2.1 copy.12
  582.2 8.0 %all-to-all-start.1 = ((f32[256,1,1024]{2,1,0:T(1,128)}), f32[256,1,1024]{2,1,0:T(1,128)}, u32[]{:S(2)}, u32[]{:S(2)}) async-start(f32[256,1,1024]{2,1,0:T(1,128)} %copy.12), calls=%async_computation.1 | async-start | bytes 2097152 | tf_op jit(solution)/shard_map/all_to_all | solution.py:52
  591.4 2.5 copy.14
  593.9 24.5 %all-to-all-done.1 = f32[256,1,1024]{2,1,0:T(1,128)} async-done(((f32[256,1,1024]{2,1,0:T(1,128)}), f32[256,1,1024]{2,1,0:T(1,128)}, u32[]{:S(2)}, u32[]{:S(2)}) %all-to-all-start.1) | async-done | bytes 1048608 | tf_op jit(solution)/shard_map/all_to_all | solution.py:52
  618.4 2.8 copy.16
  (72 shorter events, 25.4 us)
Async XLA Ops:
  7.2 358.0 %copy-start = (f32[1024,256]{1,0:T(8,128)S(1)}, f32[1024,256]{1,0:T(8,128)}, u32[]{:S(2)}) copy-start(f32[1024,256]{1,0:T(8,128)} %param.6) | copy-start | bytes 3145732
  7.2 240.7 %all-reduce.4.cloned.1.call-start = ((), (), s32[]{:S(2)}) async-start(), calls=%async_computation.2 | async-start | bytes 8388608 | tf_op jit(solution)/shard_map/psum | solution.py:25
  113.2 1.9 copy-start.1
  129.9 235.2 %all-reduce.6.cloned.1.call-start = ((), (), s32[]{:S(2)}) async-start(), calls=%async_computation.3 | async-start | bytes 8388608 | tf_op jit(solution)/shard_map/psum | solution.py:26
  582.2 36.1 %all-to-all-start.1 = ((f32[256,1,1024]{2,1,0:T(1,128)}), f32[256,1,1024]{2,1,0:T(1,128)}, u32[]{:S(2)}, u32[]{:S(2)}) async-start(f32[256,1,1024]{2,1,0:T(1,128)} %copy.12), calls=%async_computation.1 | async-start | bytes 2097152 | tf_op jit(solution)/shard_map/all_to_all | solution.py:52
Sparse Core Ops, SparseCore 0:
  130.0 117.7 all-reduce.3
  251.2 113.8 all-reduce.5
